TPU v7x, 32 devices: a whole 2x2x4 slice. The times are simulated.
32 devices in a mesh: section: 2 (over y), dp: 4 (over x, core), expert: 4 (over z).
Axes of the slice: x: 2, y: 2, z: 4, core: 2. Of those that a mesh axis runs over, the one named last changes fastest.
Arguments:
- upstream: bfloat16 [2, 256, 4096], P('section', 'expert', 'dp'), may hold values from -6 to 6
- routes: int32 [2, 256, 2], P('section', 'expert'), may hold values from 0 to 3, all different within a row; in each aligned block of 64 rows (0 to 63, 64 to 127, ..., all dimensions but the last counted through in order) at most 48 rows name the same one
- gate_weights: bfloat16 [2, 256, 2], P('section', 'expert'), may hold values from 0.049804688 to 0.5
- w_gate: bfloat16 [2, 4, 4096, 768], P('section', 'expert', 'dp'), may hold values from -0.09375 to 0.09375
- w_up: bfloat16 [2, 4, 4096, 768], P('section', 'expert', 'dp'), may hold values from -0.09375 to 0.09375
- w_down: bfloat16 [2, 4, 768, 4096], P('section', 'expert', None, 'dp'), may hold values from -0.21875 to 0.21875
- saved_gate: bfloat16 [2, 4, 4, 48, 768], P('section', 'expert'), may hold values from -6 to 6
- saved_up: bfloat16 [2, 4, 4, 48, 768], P('section', 'expert'), may hold values from -6 to 6
Outputs:
- handed: bfloat16 [2, 256, 4096], P('section', 'expert', 'dp')
- gate_grads: bfloat16 [2, 256, 2], P('section', 'expert')
Inputs may be any that keep to these rules, and one draw needn't show every extreme that they name: `routes`: each token names 2 different experts; among the 64 tokens of one device no expert is named by more than 48 tokens, and in every draw some expert is named by exactly 48 tokens of some device.
All inputs are finite; a program needn't handle non-finite values.
Results may differ from a plain program's by a relative error of at most 0.015.
Values may be sent and summed in bfloat16 or wider, within the bound.
No kernel may reach another device: no remote copies, remote signals or barrier semaphores. Data moves between devices by JAX's collectives and lax.ppermute only.
A program may use at most 64 MiB of HBM per device.

v0:
```python
import jax
import jax.numpy as jnp
from jax import lax
from jax.sharding import PartitionSpec as P


def shifted(value, axis, steps):
    count = lax.axis_size(axis)
    initial, last = (max(0, -steps), min(count, count - steps))
    return lax.ppermute(value, axis, [(source, source + steps) for source in range(initial, last)])


def slot_tables(route_block, experts, capacity):
    tokens_here, picks_here = route_block.shape
    labels = jnp.arange(experts, dtype=jnp.int32)
    onehot = (route_block[:, :, None] == labels[None, None, :]).astype(jnp.int32)
    per_token = jnp.sum(onehot, axis=1)
    earlier = jnp.cumsum(per_token, axis=0) - per_token
    slot = jnp.sum(onehot * earlier[:, None, :], axis=2)
    target = (route_block * capacity + slot).reshape(-1)
    places = jnp.arange(experts * capacity, dtype=jnp.int32)
    placement = (places[:, None] == target[None, :]).astype(jnp.bfloat16)
    by_token = jnp.sum(placement.reshape(experts * capacity, tokens_here, picks_here), axis=2)
    return (placement, by_token)


def swiglu_back(hidden_grad, gate_pre, up_pre):
    gate_val = gate_pre.astype(jnp.float32)
    up_val = up_pre.astype(jnp.float32)
    sigmoid_val = jax.nn.sigmoid(gate_val)
    silu_val = gate_val * sigmoid_val
    gate_back = (
        hidden_grad * up_val * sigmoid_val * (1.0 + gate_val * (1.0 - sigmoid_val))
    ).astype(jnp.bfloat16)
    up_back = (hidden_grad * silu_val).astype(jnp.bfloat16)
    return (gate_back, up_back)


def per_device(upstream, routes, gate_weights, w_gate, w_up, w_down, saved_gate, saved_up):
    grads_here = upstream[0]
    route_block = routes[0]
    experts = lax.axis_size("expert")
    groups = saved_gate.shape[2]
    capacity = saved_gate.shape[3]
    slot_count = groups * capacity
    feature_width = grads_here.shape[1]
    placement, by_token = slot_tables(route_block, experts, capacity)
    send_rows = jnp.dot(by_token, grads_here, preferred_element_type=jnp.float32).astype(
        jnp.bfloat16
    )
    send_gate = jnp.dot(
        placement, gate_weights[0].reshape(-1), preferred_element_type=jnp.float32
    ).astype(jnp.bfloat16)
    recv_rows, recv_gate = (
        lax.all_to_all(
            send_rows.reshape(experts, capacity, feature_width),
            "expert",
            split_axis=0,
            concat_axis=0,
            tiled=True,
        ),
        lax.all_to_all(
            send_gate.reshape(experts, capacity), "expert", split_axis=0, concat_axis=0, tiled=True
        ),
    )
    slot_rows = recv_rows.reshape(slot_count, feature_width)
    slot_gate = recv_gate.reshape(slot_count)
    gate_pre = saved_gate[0, 0].reshape(slot_count, -1)
    up_pre = saved_up[0, 0].reshape(slot_count, -1)
    down_local = w_down[0, 0]
    scaled = (slot_gate.astype(jnp.float32)[:, None] * slot_rows.astype(jnp.float32)).astype(
        jnp.bfloat16
    )
    hidden_part = lax.dot_general(
        scaled, down_local, (((1,), (1,)), ((), ())), preferred_element_type=jnp.float32
    )
    gate_val = gate_pre.astype(jnp.float32)
    hidden = (gate_val * jax.nn.sigmoid(gate_val) * up_pre.astype(jnp.float32)).astype(jnp.bfloat16)
    expert_out = jnp.dot(hidden, down_local, preferred_element_type=jnp.float32).astype(
        jnp.bfloat16
    )
    hidden_grad = lax.psum(hidden_part.astype(jnp.bfloat16), "dp").astype(jnp.float32)
    gate_back, up_back = swiglu_back(hidden_grad, gate_pre, up_pre)
    extra_back = expert_out.reshape(groups, capacity, feature_width)
    contract = (((1,), (1,)), ((), ()))
    row_grad = (
        lax.dot_general(gate_back, w_gate[0, 0], contract, preferred_element_type=jnp.float32)
        + lax.dot_general(up_back, w_up[0, 0], contract, preferred_element_type=jnp.float32)
    ).astype(jnp.bfloat16)
    back_rows, back_extra = (
        lax.all_to_all(
            row_grad.reshape(groups, capacity, feature_width),
            "expert",
            split_axis=0,
            concat_axis=0,
            tiled=True,
        ),
        lax.all_to_all(extra_back, "expert", split_axis=0, concat_axis=0, tiled=True),
    )
    inner_back = jnp.sum(
        back_extra.reshape(slot_count, feature_width).astype(jnp.float32)
        * send_rows.astype(jnp.float32),
        axis=1,
    )
    slot_back = lax.psum(inner_back.astype(jnp.bfloat16), "dp")
    routed_sum = lax.dot_general(
        by_token,
        back_rows.reshape(slot_count, feature_width),
        (((0,), (0,)), ((), ())),
        preferred_element_type=jnp.float32,
    )
    layer_grad = (grads_here.astype(jnp.float32) + routed_sum).astype(jnp.bfloat16)
    handed = shifted(layer_grad, "section", -1)
    gate_grads = (
        jnp.dot(slot_back, placement, preferred_element_type=jnp.float32)
        .astype(jnp.bfloat16)
        .reshape(route_block.shape)
    )
    return (handed[None], gate_grads[None])


def solution(mesh):
    placed = (
        P("section", "expert", "dp"),
        P("section", "expert", None),
        P("section", "expert", None),
        P("section", "expert", "dp", None),
        P("section", "expert", "dp", None),
        P("section", "expert", None, "dp"),
        P("section", "expert", None, None, None),
        P("section", "expert", None, None, None),
    )
    return jax.shard_map(
        per_device,
        mesh=mesh,
        in_specs=placed,
        out_specs=(P("section", "expert", "dp"), P("section", "expert", None)),
        check_vma=False,
    )
```

profile of v0, /device:TPU:0, one launch (start us, length us, event | category | flops | bytes accessed | tf_op | source)
XLA Modules:
  0.0 117.4 jit_solution(11747973921744513255)
XLA Ops:
  7.2 1.4 %fusion.35 = bf16[1,1,4,48,768]{4,3,2,1,0:T(8,128)(2,1)S(1)} fusion(bf16[1,1,4,48,768]{4,3,2,1,0:T(8,128)(2,1)} %param.14, bf16[1,1,4,48,768]{4,3,2,1,0:T(8,128)(2,1)} %param.15), kind=kLoop, calls=%fused_computation.39 | loop fusion | flops 1179648 | bytes 884736 | tf_op jit(solution)/shard_map/convert_element_type | solution.py:78
  8.6 0.2 copy-done
  8.8 1.2 %fusion.14 = bf16[192,1024]{1,0:T(8,128)(2,1)} fusion(bf16[192,768]{1,0:T(8,128)(2,1)S(1)} %bitcast.76, bf16[1,1,768,1024]{3,2,1,0:T(8,128)(2,1)S(1)} %copy-done), kind=kOutput, calls=%fused_computation.10 | convolution fusion | flops 302186496 | bytes 2260992 | tf_op jit(solution)/shard_map/dot_general | solution.py:79
  10.0 6.3 %all-to-all-start.3 = ((bf16[4,48,1024]{2,1,0:T(8,128)(2,1)}), bf16[4,48,1024]{2,1,0:T(8,128)(2,1)S(1)}, u32[]{:S(2)}, u32[]{:S(2)}) async-start(bf16[4,48,1024]{2,1,0:T(8,128)(2,1)} %bitcast.15), calls=%async_computation.3 | async-start | bytes 786432 | tf_op jit(solution)/shard_map/all_to_all | solution.py:98
  16.8 0.1 reshape.84
  17.0 0.1 mul.70
  17.3 0.1 reduce_sum.44
  17.4 0.1 fusion.38
  17.6 0.7 all_to_all.20
  18.4 9.7 %all-to-all-done.3 = bf16[4,48,1024]{2,1,0:T(8,128)(2,1)S(1)} async-done(((bf16[4,48,1024]{2,1,0:T(8,128)(2,1)}), bf16[4,48,1024]{2,1,0:T(8,128)(2,1)S(1)}, u32[]{:S(2)}, u32[]{:S(2)}) %all-to-all-start.3) | async-done | bytes 393248 | tf_op jit(solution)/shard_map/all_to_all | solution.py:98
  28.0 3.2 %all-to-all-start = ((bf16[4,1,48]{2,1,0:T(2,128)(2,1)}), bf16[4,1,48]{2,1,0:T(2,128)(2,1)S(1)}, u32[]{:S(2)}, u32[]{:S(2)}) async-start(bf16[4,1,48]{2,1,0:T(2,128)(2,1)} %all_to_all.20), calls=%async_computation | async-start | bytes 4096 | tf_op jit(solution)/shard_map/all_to_all | solution.py:62
  31.3 1.0 fusion.22
  32.3 4.4 %all-to-all-done = bf16[4,1,48]{2,1,0:T(2,128)(2,1)S(1)} async-done(((bf16[4,1,48]{2,1,0:T(2,128)(2,1)}), bf16[4,1,48]{2,1,0:T(2,128)(2,1)S(1)}, u32[]{:S(2)}, u32[]{:S(2)}) %all-to-all-start) | async-done | bytes 416 | tf_op jit(solution)/shard_map/all_to_all | solution.py:62
  36.7 3.5 %all-to-all-start.1 = ((bf16[4,48,1024]{2,1,0:T(8,128)(2,1)}), bf16[4,48,1024]{2,1,0:T(8,128)(2,1)S(1)}, u32[]{:S(2)}, u32[]{:S(2)}) async-start(bf16[4,48,1024]{2,1,0:T(8,128)(2,1)} %bitcast.4), calls=%async_computation.1 | async-start | bytes 786432 | tf_op jit(solution)/shard_map/all_to_all | solution.py:55
  40.2 10.0 %all-to-all-done.1 = bf16[4,48,1024]{2,1,0:T(8,128)(2,1)S(1)} async-done(((bf16[4,48,1024]{2,1,0:T(8,128)(2,1)}), bf16[4,48,1024]{2,1,0:T(8,128)(2,1)S(1)}, u32[]{:S(2)}, u32[]{:S(2)}) %all-to-all-start.1) | async-done | bytes 393248 | tf_op jit(solution)/shard_map/all_to_all | solution.py:55
  50.2 0.1 multiply_convert_fusion
  50.4 1.4 %fusion.17 = bf16[192,768]{1,0:T(8,128)(2,1)} fusion(bf16[192,1024]{1,0:T(8,128)(2,1)S(1)} %bitcast.75, bf16[1,1,768,1024]{3,2,1,0:T(8,128)(2,1)S(1)} %copy-done), kind=kOutput, calls=%fused_computation.12 | convolution fusion | flops 302137344 | bytes 2260992 | tf_op jit(solution)/shard_map/dot_general | solution.py:74
  51.8 31.7 %all-reduce.2.cloned.1.call-done = bf16[192,768]{1,0:T(8,128)(2,1)} async-done(((bf16[192,768]{1,0:T(8,128)(2,1)}), bf16[192,768]{1,0:T(8,128)(2,1)}) %all-reduce.2.cloned.1.call-update) | async-done | bytes 294928 | tf_op jit(solution)/shard_map/psum | solution.py:82
  83.5 1.4 %fusion.25 = (bf16[192,768]{1,0:T(8,128)(2,1)S(1)}, bf16[192,768]{1,0:T(8,128)(2,1)S(1)}) fusion(bf16[192,768]{1,0:T(8,128)(2,1)} %all-reduce.2.cloned.1.call-done, bf16[1,1,4,48,768]{4,3,2,1,0:T(8,128)(2,1)S(1)} %copy-done.3, bf16[1,1,4,48,768]{4,3,2,1,0:T(8,128)(2,1)} %param.15), kind=kLoop, calls=%fused_computation.24 | loop fusion | flops 2359296 | bytes 1474560 | tf_op jit(solution)/shard_map/convert_element_type | solution.py:34
  84.9 0.7 fusion
  85.5 0.7 copy-done.1
  86.3 1.4 %fusion.11 = bf16[192,1024]{1,0:T(8,128)(2,1)} fusion(f32[192,1024]{1,0:T(8,128)S(1)} %fusion, bf16[192,768]{1,0:T(8,128)(2,1)S(1)} %get-tuple-element.12, bf16[1,1,1024,768]{3,2,1,0:T(8,128)(2,1)S(1)} %copy-done.1), kind=kOutput, calls=%fused_computation.9 | convolution fusion | flops 302383104 | bytes 3047424 | tf_op jit(solution)/shard_map/dot_general | solution.py:87
  87.7 4.6 %all-to-all-start.2 = ((bf16[4,48,1024]{2,1,0:T(8,128)(2,1)}), bf16[4,48,1024]{2,1,0:T(8,128)(2,1)S(1)}, u32[]{:S(2)}, u32[]{:S(2)}) async-start(bf16[4,48,1024]{2,1,0:T(8,128)(2,1)} %bitcast.11), calls=%async_computation.2 | async-start | bytes 786432 | tf_op jit(solution)/shard_map/all_to_all | solution.py:91
  92.3 5.9 %psum.15 = bf16[192]{0:T(256)(128)(2,1)S(1)} all-reduce(bf16[192]{0:T(256)(128)(2,1)S(1)} %get-tuple-element.14), channel_id=1, replica_groups=mesh['section'=2,'dp'=4,'expert'=4] {'dp'}, use_global_device_ids=true, to_apply=%region_6.7 | all-reduce | flops 192 | bytes 768 | tf_op jit(solution)/shard_map/psum | solution.py:105
  98.2 4.7 %all-to-all-done.2 = bf16[4,48,1024]{2,1,0:T(8,128)(2,1)S(1)} async-done(((bf16[4,48,1024]{2,1,0:T(8,128)(2,1)}), bf16[4,48,1024]{2,1,0:T(8,128)(2,1)S(1)}, u32[]{:S(2)}, u32[]{:S(2)}) %all-to-all-start.2) | async-done | bytes 393248 | tf_op jit(solution)/shard_map/all_to_all | solution.py:91
  102.9 0.2 fusion.20
  103.1 1.3 %collective-permute-start = (bf16[64,1024]{1,0:T(8,128)(2,1)S(1)}, bf16[64,1024]{1,0:T(8,128)(2,1)S(1)}, u32[]{:S(2)}, u32[]{:S(2)}) collective-permute-start(bf16[64,1024]{1,0:T(8,128)(2,1)S(1)} %fusion.20), channel_id=1, source_target_pairs={{16,0},{17,1},{18,2},{19,3},{20,4},{21,5},{22,6},{23,7},{24,8},{25... | collective-permute-start | bytes 393224 | tf_op jit(solution)/shard_map/ppermute | solution.py:10
  104.4 0.1 fusion.21
  104.5 0.2 broadcast_in_dim_reshape.4
  104.7 0.6 copy.42
  105.3 4.6 %collective-permute-done = bf16[64,1024]{1,0:T(8,128)(2,1)S(1)} collective-permute-done((bf16[64,1024]{1,0:T(8,128)(2,1)S(1)}, bf16[64,1024]{1,0:T(8,128)(2,1)S(1)}, u32[]{:S(2)}, u32[]{:S(2)}) %collective-permute-start) | collective-permute-done | bytes 131104 | tf_op jit(solution)/shard_map/ppermute | solution.py:10
  109.9 0.7 copy.45
  (32 shorter events, 0.8 us)
Async XLA Ops:
  7.2 1.6 %copy-start = (bf16[1,1,768,1024]{3,2,1,0:T(8,128)(2,1)S(1)}, bf16[1,1,768,1024]{3,2,1,0:T(8,128)(2,1)}, u32[]{:S(2)}) copy-start(bf16[1,1,768,1024]{3,2,1,0:T(8,128)(2,1)} %param.13) | copy-start | bytes 4718596
  8.5 7.8 %copy-start.6 = (s32[1,64,2]{1,2,0:T(2,128)S(1)}, s32[1,64,2]{1,2,0:T(2,128)}, u32[]{:S(2)}) copy-start(s32[1,64,2]{1,2,0:T(2,128)} %param.9) | copy-start | bytes 1540
  8.8 7.9 %copy-start.7 = (bf16[1,64,2]{1,2,0:T(2,128)(2,1)S(1)}, bf16[1,64,2]{1,2,0:T(2,128)(2,1)}, u32[]{:S(2)}) copy-start(bf16[1,64,2]{1,2,0:T(2,128)(2,1)} %param.10) | copy-start | bytes 772
  8.8 22.5 %copy-start.4 = (bf16[1,64,1024]{2,1,0:T(8,128)(2,1)S(1)}, bf16[1,64,1024]{2,1,0:T(8,128)(2,1)}, u32[]{:S(2)}) copy-start(bf16[1,64,1024]{2,1,0:T(8,128)(2,1)} %param.8) | copy-start | bytes 393220
  10.0 18.0 %all-to-all-start.3 = ((bf16[4,48,1024]{2,1,0:T(8,128)(2,1)}), bf16[4,48,1024]{2,1,0:T(8,128)(2,1)S(1)}, u32[]{:S(2)}, u32[]{:S(2)}) async-start(bf16[4,48,1024]{2,1,0:T(8,128)(2,1)} %bitcast.15), calls=%async_computation.3 | async-start | bytes 786432 | tf_op jit(solution)/shard_map/all_to_all | solution.py:98
  28.0 8.7 %all-to-all-start = ((bf16[4,1,48]{2,1,0:T(2,128)(2,1)}), bf16[4,1,48]{2,1,0:T(2,128)(2,1)S(1)}, u32[]{:S(2)}, u32[]{:S(2)}) async-start(bf16[4,1,48]{2,1,0:T(2,128)(2,1)} %all_to_all.20), calls=%async_computation | async-start | bytes 4096 | tf_op jit(solution)/shard_map/all_to_all | solution.py:62
  36.7 13.5 %all-to-all-start.1 = ((bf16[4,48,1024]{2,1,0:T(8,128)(2,1)}), bf16[4,48,1024]{2,1,0:T(8,128)(2,1)S(1)}, u32[]{:S(2)}, u32[]{:S(2)}) async-start(bf16[4,48,1024]{2,1,0:T(8,128)(2,1)} %bitcast.4), calls=%async_computation.1 | async-start | bytes 786432 | tf_op jit(solution)/shard_map/all_to_all | solution.py:55
  40.2 43.3 %all-reduce.2.cloned.1.call-start = ((), (), s32[]{:S(2)}) async-start(), calls=%async_computation.4 | async-start | bytes 589824 | tf_op jit(solution)/shard_map/psum | solution.py:82
  50.2 33.2 %copy-start.3 = (bf16[1,1,4,48,768]{4,3,2,1,0:T(8,128)(2,1)S(1)}, bf16[1,1,4,48,768]{4,3,2,1,0:T(8,128)(2,1)}, u32[]{:S(2)}) copy-start(bf16[1,1,4,48,768]{4,3,2,1,0:T(8,128)(2,1)} %param.14) | copy-start | bytes 884740
  50.4 34.5 %copy-start.2 = (bf16[1,1,1024,768]{3,2,1,0:T(8,128)(2,1)S(1)}, bf16[1,1,1024,768]{3,2,1,0:T(8,128)(2,1)}, u32[]{:S(2)}) copy-start(bf16[1,1,1024,768]{3,2,1,0:T(8,128)(2,1)} %param.12) | copy-start | bytes 4718596
  84.9 1.4 %copy-start.1 = (bf16[1,1,1024,768]{3,2,1,0:T(8,128)(2,1)S(1)}, bf16[1,1,1024,768]{3,2,1,0:T(8,128)(2,1)}, u32[]{:S(2)}) copy-start(bf16[1,1,1024,768]{3,2,1,0:T(8,128)(2,1)} %param.11) | copy-start | bytes 4718596
  86.3 16.6 %copy-start.5 = (bf16[1,64,1024]{2,1,0:T(8,128)(2,1)S(1)}, bf16[1,64,1024]{2,1,0:T(8,128)(2,1)}, u32[]{:S(2)}) copy-start(bf16[1,64,1024]{2,1,0:T(8,128)(2,1)} %param.8) | copy-start | bytes 393220
  87.7 15.2 %all-to-all-start.2 = ((bf16[4,48,1024]{2,1,0:T(8,128)(2,1)}), bf16[4,48,1024]{2,1,0:T(8,128)(2,1)S(1)}, u32[]{:S(2)}, u32[]{:S(2)}) async-start(bf16[4,48,1024]{2,1,0:T(8,128)(2,1)} %bitcast.11), calls=%async_computation.2 | async-start | bytes 786432 | tf_op jit(solution)/shard_map/all_to_all | solution.py:91
  103.1 6.9 %collective-permute-start = (bf16[64,1024]{1,0:T(8,128)(2,1)S(1)}, bf16[64,1024]{1,0:T(8,128)(2,1)S(1)}, u32[]{:S(2)}, u32[]{:S(2)}) collective-permute-start(bf16[64,1024]{1,0:T(8,128)(2,1)S(1)} %fusion.20), channel_id=1, source_target_pairs={{16,0},{17,1},{18,2},{19,3},{20,4},{21,5},{22,6},{23,7},{24,8},{25... | collective-permute-start | bytes 393224 | tf_op jit(solution)/shard_map/ppermute | solution.py:10
Sparse Core Ops, SparseCore 0:
  51.9 31.5 all-reduce.1
where the time goes:
time: 118 us; the launch traced here: 117 us
  waiting for transfers between devices  65.1 us (55%)
  starting transfers between devices  19 us (16%)
  between operations  14.2 us (12%)
  matrix products  6.17 us (5%)
  blocking collectives  5.93 us (5%)
  local copies, waits for them, and re-layouts  4 us (3%)
  other arithmetic  3.1 us (3%)
    psum x1, waiting for transfers between devices, per_device(): lax.psum(hidden_part.astype(jnp.bfloat16), 'dp').astype(jnp.float32)  31.7 us
    all_to_all x1, waiting for transfers between devices, per_device(): lax.all_to_all(send_rows.reshape(experts, capacity, feature_width), 'expe...  10 us
    all_to_all x1, waiting for transfers between devices, per_device(): lax.all_to_all(extra_back, 'expert', split_axis=0, concat_axis=0, tiled=T...  9.65 us
    all_to_all x1, starting transfers between devices, per_device(): lax.all_to_all(extra_back, 'expert', split_axis=0, concat_axis=0, tiled=T...  6.35 us
    psum x1, blocking collectives, per_device(): slot_back = lax.psum(inner_back.astype(jnp.bfloat16), 'dp')  5.93 us
    all_to_all x1, waiting for transfers between devices, per_device(): lax.all_to_all(row_grad.reshape(groups, capacity, feature_width), 'expert...  4.65 us
    ppermute x1, waiting for transfers between devices, shifted(): lax.ppermute(value, axis, [(source, source + steps) for source in range(i...  4.65 us
    all_to_all x1, starting transfers between devices, per_device(): lax.all_to_all(row_grad.reshape(groups, capacity, feature_width), 'expert...  4.6 us
  transfers between devices with their start and end apart: 6, of which 6 were waited for; matrix products, arithmetic and copies ran while one was open for 3% of the time, Pallas kernels for 0%

commit v1 on v0

--- a/solution.py
+++ b/solution.py
@@ -79,7 +79,9 @@
     expert_out = jnp.dot(hidden, down_local, preferred_element_type=jnp.float32).astype(
         jnp.bfloat16
     )
-    hidden_grad = lax.psum(hidden_part.astype(jnp.bfloat16), "dp").astype(jnp.float32)
+    hidden_grad = jnp.sum(lax.all_gather(hidden_part.astype(jnp.bfloat16), "dp"), axis=0).astype(
+        jnp.float32
+    )
     gate_back, up_back = swiglu_back(hidden_grad, gate_pre, up_pre)
     extra_back = expert_out.reshape(groups, capacity, feature_width)
     contract = (((1,), (1,)), ((), ()))

time: 118 us -> 107 us (0.907)
  waiting for transfers between devices: 65.1 us -> 46.5 us
  other arithmetic: 3.1 us -> 7.12 us
  matrix products: 6.17 us -> 8.65 us
    psum x1 -> x0, waiting for transfers between devices: 31.7 us -> none  [per_device(): lax.psum(hidden_part.astype(jnp.bfloat16), 'dp').astype(jnp.float32)]
    all_gather x0 -> x1, waiting for transfers between devices: none -> 16.7 us  [per_device(): lax.all_gather(hidden_part.astype(jnp.bfloat16), 'dp')]
    all_to_all x1, starting transfers between devices: 3.22 us -> 6.35 us  [per_device(): lax.all_to_all(send_gate.reshape(experts, capacity), 'expert', split_axis...]
    reduce_sum x0 -> x2, other arithmetic: none -> 2.7 us  [the longest x1 1.52 us: per_device(): jnp.sum(lax.all_gather(hidden_part.astype(jnp.bfloat16), 'dp'), axis=0)]
    all_to_all x1, waiting for transfers between devices: 4.43 us -> 2.23 us  [per_device(): lax.all_to_all(send_gate.reshape(experts, capacity), 'expert', split_axis...]
    all_to_all x1, starting transfers between devices: 6.35 us -> 4.73 us  [per_device(): lax.all_to_all(extra_back, 'expert', split_axis=0, concat_axis=0, tiled=T...]
    dot_general x1, matrix products: 0.66 us -> 2.21 us  [per_device(): lax.dot_general(up_back, w_up[0, 0], contract, preferred_element_type=jnp...]
    convert_element_type x1 -> x0, other arithmetic: 1.37 us -> none  [swiglu_back(): gate_back = (hidden_grad * up_val * sigmoid_val * (1.0 + gate_val * (1.0...]
  transfers between devices with their start and end apart: 6 -> 6, of which waited for: 6 -> 6; matrix products, arithmetic and copies ran while one was open for 3% -> 8% of each run, Pallas kernels for 0% -> 0%
where the time goes in v1:
time: 107 us; the launch traced here: 106 us
  waiting for transfers between devices  46.5 us (43%)
  starting transfers between devices  19.3 us (18%)
  between operations  14.2 us (13%)
  matrix products  8.65 us (8%)
  other arithmetic  7.12 us (7%)
  blocking collectives  5.98 us (6%)
  local copies, waits for them, and re-layouts  4.32 us (4%)
    all_gather x1, waiting for transfers between devices, per_device(): lax.all_gather(hidden_part.astype(jnp.bfloat16), 'dp')  16.7 us
    all_to_all x1, waiting for transfers between devices, per_device(): lax.all_to_all(send_rows.reshape(experts, capacity, feature_width), 'expe...  10.5 us
    all_to_all x1, waiting for transfers between devices, per_device(): lax.all_to_all(extra_back, 'expert', split_axis=0, concat_axis=0, tiled=T...  8.41 us
    all_to_all x1, starting transfers between devices, per_device(): lax.all_to_all(send_gate.reshape(experts, capacity), 'expert', split_axis...  6.35 us
    psum x1, blocking collectives, per_device(): slot_back = lax.psum(inner_back.astype(jnp.bfloat16), 'dp')  5.98 us
    all_to_all x1, starting transfers between devices, per_device(): lax.all_to_all(extra_back, 'expert', split_axis=0, concat_axis=0, tiled=T...  4.73 us
    ppermute x1, waiting for transfers between devices, shifted(): lax.ppermute(value, axis, [(source, source + steps) for source in range(i...  4.65 us
    all_to_all x1, waiting for transfers between devices, per_device(): lax.all_to_all(row_grad.reshape(groups, capacity, feature_width), 'expert...  4.04 us
  transfers between devices with their start and end apart: 6, of which 6 were waited for; matrix products, arithmetic and copies ran while one was open for 8% of the time, Pallas kernels for 0%

profile of v1, /device:TPU:0, one launch (start us, length us, event | category | flops | bytes accessed | tf_op | source)
XLA Modules:
  0.0 106.1 jit_solution(10828815765891260589)
XLA Ops:
  7.2 0.8 broadcast_multiply_fusion
  8.0 0.7 convert_reduce_fusion
  8.7 0.8 copy.40
  9.4 0.1 reshape.95
  10.1 0.7 select_reduce_fusion
  11.2 0.7 all_to_all.20
  11.9 6.3 %all-to-all-start = ((bf16[4,1,48]{2,1,0:T(2,128)(2,1)}), bf16[4,1,48]{2,1,0:T(2,128)(2,1)S(1)}, u32[]{:S(2)}, u32[]{:S(2)}) async-start(bf16[4,1,48]{2,1,0:T(2,128)(2,1)} %all_to_all.20), calls=%async_computation | async-start | bytes 4096 | tf_op jit(solution)/shard_map/all_to_all | solution.py:62
  18.3 0.7 multiply_add_fusion
  19.0 0.6 copy-done.6
  19.7 1.9 %convolution_convert_fusion = bf16[192,1024]{1,0:T(8,128)(2,1)} fusion(bf16[192,64]{0,1:T(8,128)(2,1)S(1)} %fusion.35, bf16[1,64,1024]{2,1,0:T(8,128)(2,1)} %param.8), kind=kOutput, calls=%fused_computation.11 | convolution fusion | flops 25362432 | bytes 548864 | tf_op jit(solution)/shard_map/dot_general | solution.py:48
  21.6 2.2 %all-to-all-done = bf16[4,1,48]{2,1,0:T(2,128)(2,1)S(1)} async-done(((bf16[4,1,48]{2,1,0:T(2,128)(2,1)}), bf16[4,1,48]{2,1,0:T(2,128)(2,1)S(1)}, u32[]{:S(2)}, u32[]{:S(2)}) %all-to-all-start) | async-done | bytes 416 | tf_op jit(solution)/shard_map/all_to_all | solution.py:62
  23.8 3.5 %all-to-all-start.1 = ((bf16[4,48,1024]{2,1,0:T(8,128)(2,1)}), bf16[4,48,1024]{2,1,0:T(8,128)(2,1)S(1)}, u32[]{:S(2)}, u32[]{:S(2)}) async-start(bf16[4,48,1024]{2,1,0:T(8,128)(2,1)} %bitcast.4), calls=%async_computation.1 | async-start | bytes 786432 | tf_op jit(solution)/shard_map/all_to_all | solution.py:55
  27.4 10.5 %all-to-all-done.1 = bf16[4,48,1024]{2,1,0:T(8,128)(2,1)S(1)} async-done(((bf16[4,48,1024]{2,1,0:T(8,128)(2,1)}), bf16[4,48,1024]{2,1,0:T(8,128)(2,1)S(1)}, u32[]{:S(2)}, u32[]{:S(2)}) %all-to-all-start.1) | async-done | bytes 393248 | tf_op jit(solution)/shard_map/all_to_all | solution.py:55
  38.0 1.4 %fusion.17 = bf16[192,768]{1,0:T(8,128)(2,1)} fusion(bf16[192,1024]{1,0:T(8,128)(2,1)S(1)} %bitcast.57, bf16[1,1,768,1024]{3,2,1,0:T(8,128)(2,1)S(1)} %copy-done), kind=kOutput, calls=%fused_computation.12 | convolution fusion | flops 302137344 | bytes 2260992 | tf_op jit(solution)/shard_map/dot_general | solution.py:74
  39.4 16.7 %all-gather.3.cloned.1.call-done = bf16[768,768]{1,0:T(8,128)(2,1)} async-done(((bf16[192,768]{1,0:T(8,128)(2,1)}), bf16[768,768]{1,0:T(8,128)(2,1)}) %all-gather.3.cloned.1.call-update) | async-done | bytes 1179664 | tf_op jit(solution)/shard_map/all_gather | solution.py:82
  56.1 1.5 %reduce_sum.57 = bf16[192,768]{1,0:T(8,128)(2,1)S(1)} reduce(bf16[4,192,768]{2,1,0:T(8,128)(2,1)} %bitcast.62, bf16[]{:T(256)} %constant.12.clone.1), dimensions={0}, to_apply=%region_4.5 | reduce | flops 442368 | bytes 1474562 | tf_op jit(solution)/shard_map/reduce_sum | solution.py:82
  57.6 1.2 %fusion.23 = (bf16[1,1,4,48,768]{4,3,2,1,0:T(8,128)(2,1)S(1)}, bf16[1,1,4,48,768]{4,3,2,1,0:T(8,128)(2,1)}, bf16[1,1,4,48,768]{4,3,2,1,0:T(8,128)(2,1)}) fusion(bf16[1,1,4,48,768]{4,3,2,1,0:T(8,128)(2,1)S(1)} %copy-done.4, bf16[1,1,4,48,768]{4,3,2,1,0:T(8,128)(2,1)S(1)} %copy-done.5, bf16[1,1,4,48,768]{4,3,2,1,0:T(8,128)(2,1)S(1)} %bitcast.61), kind=kLoop, calls=%fused_computation.26 | loop fusion | flops 2654208 | bytes 1769472 | tf_op jit(solution)/shard_map/convert_element_type | solution.py:78
  58.8 1.2 %fusion.14 = bf16[192,1024]{1,0:T(8,128)(2,1)} fusion(bf16[192,768]{1,0:T(8,128)(2,1)S(1)} %bitcast.59, bf16[1,1,768,1024]{3,2,1,0:T(8,128)(2,1)S(1)} %copy-done), kind=kOutput, calls=%fused_computation.10 | convolution fusion | flops 302186496 | bytes 2260992 | tf_op jit(solution)/shard_map/dot_general | solution.py:79
  60.1 4.7 %all-to-all-start.3 = ((bf16[4,48,1024]{2,1,0:T(8,128)(2,1)}), bf16[4,48,1024]{2,1,0:T(8,128)(2,1)S(1)}, u32[]{:S(2)}, u32[]{:S(2)}) async-start(bf16[4,48,1024]{2,1,0:T(8,128)(2,1)} %bitcast.56), calls=%async_computation.3 | async-start | bytes 786432 | tf_op jit(solution)/shard_map/all_to_all | solution.py:100
  64.8 2.2 %fusion = f32[192,1024]{1,0:T(8,128)S(1)} fusion(bf16[192,768]{1,0:T(8,128)(2,1)} %bitcast.60, bf16[1,1,1024,768]{3,2,1,0:T(8,128)(2,1)} %param.12), kind=kOutput, calls=%fused_computation | convolution fusion | flops 301989888 | bytes 2654208 | tf_op jit(solution)/shard_map/dot_general | solution.py:90
  67.0 1.4 %fusion.11 = bf16[192,1024]{1,0:T(8,128)(2,1)} fusion(f32[192,1024]{1,0:T(8,128)S(1)} %fusion, bf16[192,768]{1,0:T(8,128)(2,1)S(1)} %bitcast.58, bf16[1,1,1024,768]{3,2,1,0:T(8,128)(2,1)S(1)} %copy-done.1), kind=kOutput, calls=%fused_computation.9 | convolution fusion | flops 302383104 | bytes 3047424 | tf_op jit(solution)/shard_map/dot_general | solution.py:89
  68.4 8.4 %all-to-all-done.3 = bf16[4,48,1024]{2,1,0:T(8,128)(2,1)S(1)} async-done(((bf16[4,48,1024]{2,1,0:T(8,128)(2,1)}), bf16[4,48,1024]{2,1,0:T(8,128)(2,1)S(1)}, u32[]{:S(2)}, u32[]{:S(2)}) %all-to-all-start.3) | async-done | bytes 393248 | tf_op jit(solution)/shard_map/all_to_all | solution.py:100
  76.9 3.5 %all-to-all-start.2 = ((bf16[4,48,1024]{2,1,0:T(8,128)(2,1)}), bf16[4,48,1024]{2,1,0:T(8,128)(2,1)S(1)}, u32[]{:S(2)}, u32[]{:S(2)}) async-start(bf16[4,48,1024]{2,1,0:T(8,128)(2,1)} %bitcast.14), calls=%async_computation.2 | async-start | bytes 786432 | tf_op jit(solution)/shard_map/all_to_all | solution.py:93
  80.3 1.2 %fusion.22 = bf16[192]{0:T(256)(128)(2,1)S(1)} fusion(bf16[192,1024]{1,0:T(8,128)(2,1)S(1)} %bitcast.54, bf16[192,1024]{1,0:T(8,128)(2,1)} %convolution_convert_fusion), kind=kLoop, calls=%fused_computation.21 | loop fusion | flops 786240 | bytes 786816 | tf_op jit(solution)/shard_map/reduce_sum | solution.py:102
  81.5 6.0 %psum.7 = bf16[192]{0:T(256)(128)(2,1)S(1)} all-reduce(bf16[192]{0:T(256)(128)(2,1)S(1)} %fusion.22), channel_id=1, replica_groups=mesh['section'=2,'dp'=4,'expert'=4] {'dp'}, use_global_device_ids=true, to_apply=%region_6.7 | all-reduce | flops 192 | bytes 768 | tf_op jit(solution)/shard_map/psum | solution.py:107
  87.5 4.0 %all-to-all-done.2 = bf16[4,48,1024]{2,1,0:T(8,128)(2,1)S(1)} async-done(((bf16[4,48,1024]{2,1,0:T(8,128)(2,1)}), bf16[4,48,1024]{2,1,0:T(8,128)(2,1)S(1)}, u32[]{:S(2)}, u32[]{:S(2)}) %all-to-all-start.2) | async-done | bytes 393248 | tf_op jit(solution)/shard_map/all_to_all | solution.py:93
  91.5 0.2 fusion.20
  91.7 1.3 %collective-permute-start = (bf16[64,1024]{1,0:T(8,128)(2,1)S(1)}, bf16[64,1024]{1,0:T(8,128)(2,1)S(1)}, u32[]{:S(2)}, u32[]{:S(2)}) collective-permute-start(bf16[64,1024]{1,0:T(8,128)(2,1)S(1)} %fusion.20), channel_id=1, source_target_pairs={{16,0},{17,1},{18,2},{19,3},{20,4},{21,5},{22,6},{23,7},{24,8},{25... | collective-permute-start | bytes 393224 | tf_op jit(solution)/shard_map/ppermute | solution.py:10
  93.2 0.2 broadcast_in_dim_reshape.4
  93.3 0.6 copy.42
  94.0 4.6 %collective-permute-done = bf16[64,1024]{1,0:T(8,128)(2,1)S(1)} collective-permute-done((bf16[64,1024]{1,0:T(8,128)(2,1)S(1)}, bf16[64,1024]{1,0:T(8,128)(2,1)S(1)}, u32[]{:S(2)}, u32[]{:S(2)}) %collective-permute-start) | collective-permute-done | bytes 131104 | tf_op jit(solution)/shard_map/ppermute | solution.py:10
  98.6 0.7 copy.44
  (33 shorter events, 1.4 us)
Async XLA Ops:
  7.2 30.8 %copy-start = (bf16[1,1,768,1024]{3,2,1,0:T(8,128)(2,1)S(1)}, bf16[1,1,768,1024]{3,2,1,0:T(8,128)(2,1)}, u32[]{:S(2)}) copy-start(bf16[1,1,768,1024]{3,2,1,0:T(8,128)(2,1)} %param.13) | copy-start | bytes 4718596
  11.9 11.9 %all-to-all-start = ((bf16[4,1,48]{2,1,0:T(2,128)(2,1)}), bf16[4,1,48]{2,1,0:T(2,128)(2,1)S(1)}, u32[]{:S(2)}, u32[]{:S(2)}) async-start(bf16[4,1,48]{2,1,0:T(2,128)(2,1)} %all_to_all.20), calls=%async_computation | async-start | bytes 4096 | tf_op jit(solution)/shard_map/all_to_all | solution.py:62
  19.0 0.6 copy-start.6
  23.8 14.0 %all-to-all-start.1 = ((bf16[4,48,1024]{2,1,0:T(8,128)(2,1)}), bf16[4,48,1024]{2,1,0:T(8,128)(2,1)S(1)}, u32[]{:S(2)}, u32[]{:S(2)}) async-start(bf16[4,48,1024]{2,1,0:T(8,128)(2,1)} %bitcast.4), calls=%async_computation.1 | async-start | bytes 786432 | tf_op jit(solution)/shard_map/all_to_all | solution.py:55
  27.3 28.8 %all-gather.3.cloned.1.call-start = ((), (), s32[]{:S(2)}) async-start(), calls=%async_computation.4 | async-start | bytes 1474560 | tf_op jit(solution)/shard_map/all_gather | solution.py:82
  38.0 19.7 %copy-start.4 = (bf16[1,1,4,48,768]{4,3,2,1,0:T(8,128)(2,1)S(1)}, bf16[1,1,4,48,768]{4,3,2,1,0:T(8,128)(2,1)}, u32[]{:S(2)}) copy-start(bf16[1,1,4,48,768]{4,3,2,1,0:T(8,128)(2,1)} %param.15) | copy-start | bytes 884740
  38.0 19.6 %copy-start.5 = (bf16[1,1,4,48,768]{4,3,2,1,0:T(8,128)(2,1)S(1)}, bf16[1,1,4,48,768]{4,3,2,1,0:T(8,128)(2,1)}, u32[]{:S(2)}) copy-start(bf16[1,1,4,48,768]{4,3,2,1,0:T(8,128)(2,1)} %param.14) | copy-start | bytes 884740
  60.1 6.9 %copy-start.1 = (bf16[1,1,1024,768]{3,2,1,0:T(8,128)(2,1)S(1)}, bf16[1,1,1024,768]{3,2,1,0:T(8,128)(2,1)}, u32[]{:S(2)}) copy-start(bf16[1,1,1024,768]{3,2,1,0:T(8,128)(2,1)} %param.11) | copy-start | bytes 4718596
  60.1 16.8 %all-to-all-start.3 = ((bf16[4,48,1024]{2,1,0:T(8,128)(2,1)}), bf16[4,48,1024]{2,1,0:T(8,128)(2,1)S(1)}, u32[]{:S(2)}, u32[]{:S(2)}) async-start(bf16[4,48,1024]{2,1,0:T(8,128)(2,1)} %bitcast.56), calls=%async_computation.3 | async-start | bytes 786432 | tf_op jit(solution)/shard_map/all_to_all | solution.py:100
  64.8 2.2 %copy-start.2 = (bf16[1,1,4,48,768]{4,3,2,1,0:T(8,128)(2,1)S(1)}, bf16[1,1,4,48,768]{4,3,2,1,0:T(8,128)(2,1)}, u32[]{:S(2)}) copy-start(bf16[1,1,4,48,768]{4,3,2,1,0:T(8,128)(2,1)} %get-tuple-element.13) | copy-start | bytes 884740
  68.4 23.1 %copy-start.3 = (bf16[1,64,1024]{2,1,0:T(8,128)(2,1)S(1)}, bf16[1,64,1024]{2,1,0:T(8,128)(2,1)}, u32[]{:S(2)}) copy-start(bf16[1,64,1024]{2,1,0:T(8,128)(2,1)} %param.8) | copy-start | bytes 393220
  68.4 23.1 %copy-start.7 = (bf16[192,64]{0,1:T(8,128)(2,1)S(1)}, bf16[192,64]{0,1:T(8,128)(2,1)}, u32[]{:S(2)}) copy-start(bf16[192,64]{0,1:T(8,128)(2,1)} %copy-done.6) | copy-start | bytes 73732
  76.9 14.7 %all-to-all-start.2 = ((bf16[4,48,1024]{2,1,0:T(8,128)(2,1)}), bf16[4,48,1024]{2,1,0:T(8,128)(2,1)S(1)}, u32[]{:S(2)}, u32[]{:S(2)}) async-start(bf16[4,48,1024]{2,1,0:T(8,128)(2,1)} %bitcast.14), calls=%async_computation.2 | async-start | bytes 786432 | tf_op jit(solution)/shard_map/all_to_all | solution.py:93
  91.7 6.9 %collective-permute-start = (bf16[64,1024]{1,0:T(8,128)(2,1)S(1)}, bf16[64,1024]{1,0:T(8,128)(2,1)S(1)}, u32[]{:S(2)}, u32[]{:S(2)}) collective-permute-start(bf16[64,1024]{1,0:T(8,128)(2,1)S(1)} %fusion.20), channel_id=1, source_target_pairs={{16,0},{17,1},{18,2},{19,3},{20,4},{21,5},{22,6},{23,7},{24,8},{25... | collective-permute-start | bytes 393224 | tf_op jit(solution)/shard_map/ppermute | solution.py:10
Sparse Core Ops, SparseCore 0:
  39.5 16.5 all-gather.2
